TPU v7x, 512 devices: a whole 4x4x16 slice. The times are simulated.
512 devices in a mesh: prow: 16 (over x, y), pcol: 32 (over z, core).
Axes of the slice: x: 4, y: 4, z: 16, core: 2. Of those that a mesh axis runs over, the one named last changes fastest.
Arguments:
- adjoint_trail: float32 [2, 16, 256, 1, 32, 256], P(None, 'prow', None, None, 'pcol'), as said below
- factor_low: float32 [2, 16, 32, 8, 4, 256], P(None, 'prow', 'pcol'), may hold values from -0.0625 to 0.0625
- adjoint_low: float32 [2, 16, 32, 8, 4, 256], P(None, 'prow', 'pcol'), may hold values from -6 to 6
- factor_top: float32 [10, 256, 256], P(None, 'pcol'), as said below
- adjoint_top: float32 [10, 256, 256], P(None, 'pcol'), may hold values from -6 to 6
- diag_inverse: float32 [4, 256, 256], P(None, 'pcol'), as said below
Outputs:
- grad_low: float32 [2, 16, 32, 8, 4, 256], P(None, 'prow', 'pcol')
- grad_top: float32 [10, 256, 256], P(None, 'pcol')
Inputs may be any that keep to these rules, and one draw needn't show every extreme that they name: adjoint_trail reshaped row-major to 8192 x 8192 is symmetric. The diagonal blocks factor_top[j (j + 1) / 2 + j] are lower triangular with a positive diagonal. diag_inverse[j] is the inverse of factor_top[j (j + 1) / 2 + j].
All inputs are finite; a program needn't handle non-finite values.
Results may differ from a plain program's by a relative error of at most 0.00024.
Values sent between devices are 32-bit elements; how exact they have to be, the bound alone decides.
A program may use at most 64 MiB of HBM per device.

v0:
```python
import jax
import jax.numpy as jnp
from jax import lax
from jax.sharding import PartitionSpec as P

NB = 256
K = 4


HIGHEST = lax.Precision.HIGHEST


def from_root(array, axis, root):
    mine = lax.axis_index(axis) == root
    return lax.psum(jnp.where(mine, array, jnp.zeros_like(array)), axis)


def matmul(left, right):
    return jnp.dot(left, right, precision=HIGHEST, preferred_element_type=jnp.float32)


def inner_product(left, right):
    return lax.dot_general(
        left, right, (((0,), (0,)), ((), ())), precision=HIGHEST, preferred_element_type=jnp.float32
    )


def block_slot(row_block, col_block):
    return row_block * (row_block + 1) // 2 + col_block


def half_lower(square):
    size = square.shape[0]
    row_ids = lax.broadcasted_iota(jnp.int32, (size, size), 0)
    col_ids = lax.broadcasted_iota(jnp.int32, (size, size), 1)
    return jnp.where(row_ids > col_ids, square, jnp.where(row_ids == col_ids, 0.5 * square, 0.0))


def diagonal_adjoint(diagonal, inverse, lower_adj):
    inner = half_lower(inner_product(jnp.tril(diagonal), lower_adj))
    spread = inner_product(inverse, matmul(inner, inverse))
    return 0.5 * (spread + spread.T)


def rows_one(piece):
    return lax.all_gather(piece, "pcol", axis=1, tiled=True)


def owner_one(piece, root):
    return from_root(piece, "prow", root)


def reduce_one(term, count):
    return lax.psum_scatter(
        term(jnp.int32(0), lax.axis_size("pcol") * count), "pcol", scatter_dimension=0, tiled=True
    )


def trailing_product(trail, panels, gather_rows, send_owner, reduce_rows):
    prow_count = lax.axis_size("prow")
    pcol_count = lax.axis_size("pcol")
    cycles, sub_rows, width = panels.shape
    block = sub_rows * pcol_count
    gathered = gather_rows(panels[:, None]).reshape(cycles, block, width)
    column = lax.axis_index("pcol")
    col_cycles = trail.shape[3]
    global_block = 0 + column
    share = lax.dynamic_index_in_dim(gathered, global_block // prow_count, 0, keepdims=False)
    owned = [send_owner(share, global_block % prow_count)]
    stacked = jnp.stack(owned)
    view = trail.reshape(cycles, pcol_count, sub_rows, col_cycles, block)
    unit = cycles * sub_rows

    def term(start, count):
        product = jnp.einsum(
            "iaekb,kbn->aien", view, stacked, precision=HIGHEST, preferred_element_type=jnp.float32
        )
        return product.reshape(count, width)

    return reduce_rows(term, unit).reshape(cycles, sub_rows, width)


def per_device(adjoint_trail, factor_low, adjoint_low, factor_top, adjoint_top, diag_inverse):
    cycles = factor_low.shape[0]
    sub_rows = factor_low.shape[3]
    local_rows = cycles * sub_rows
    low_factor = factor_low.reshape(cycles, sub_rows, K * NB)
    low_adjoint = adjoint_low.reshape(local_rows, K, NB)
    columns = low_factor.reshape(local_rows, K, NB)
    top_factor, top_adjoint, inverses = (
        lax.all_gather(factor_top, "pcol", axis=1, tiled=True),
        lax.all_gather(adjoint_top, "pcol", axis=1, tiled=True),
        lax.all_gather(diag_inverse, "pcol", axis=1, tiled=True),
    )
    lower_grads = [None] * K
    diag_grads = [None] * K
    upper_grads = {}
    grams = {}

    def lower_step(panel):
        single = low_factor[:, :, panel * NB : (panel + 1) * NB]
        image = trailing_product(adjoint_trail, single, rows_one, owner_one, reduce_one).reshape(
            local_rows, NB
        )
        residual = low_adjoint[:, panel] - 2.0 * image
        for later in range(panel + 1, K):
            residual = residual - matmul(lower_grads[later], top_factor[block_slot(later, panel)])
        lower_grads[panel] = matmul(residual, inverses[panel])

    def top_step(panel):
        for row_block in range(panel + 1, K):
            top_residual = top_adjoint[block_slot(row_block, panel)] - grams[row_block, panel]
            top_residual = top_residual - 2.0 * matmul(
                diag_grads[row_block], top_factor[block_slot(row_block, panel)]
            )
            for middle in range(panel + 1, row_block):
                top_residual = top_residual - matmul(
                    upper_grads[middle, row_block], top_factor[block_slot(middle, panel)]
                )
            for beyond in range(row_block + 1, K):
                top_residual = top_residual - inner_product(
                    upper_grads[row_block, beyond], top_factor[block_slot(beyond, panel)]
                )
            upper_grads[panel, row_block] = matmul(top_residual, inverses[panel])
        lower_adj = top_adjoint[block_slot(panel, panel)] - grams[panel, panel]
        for row_block in range(panel + 1, K):
            lower_adj = lower_adj - inner_product(
                upper_grads[panel, row_block], top_factor[block_slot(row_block, panel)]
            )
        diag_grads[panel] = diagonal_adjoint(
            top_factor[block_slot(panel, panel)], inverses[panel], jnp.tril(lower_adj)
        )

    for panel in reversed(range(K)):
        lower_step(panel)
        local_gram = jnp.stack(
            [inner_product(lower_grads[panel], columns[:, earlier]) for earlier in range(panel + 1)]
        )
        summed = lax.psum(local_gram, ("prow", "pcol"))
        for earlier in range(panel + 1):
            grams[panel, earlier] = summed[earlier]
        top_step(panel)
    grad_low = jnp.stack(lower_grads, 1).reshape(factor_low.shape)
    blocks = []
    for row_block in range(K):
        for col_block in range(row_block + 1):
            if row_block == col_block:
                blocks.append(diag_grads[col_block])
            else:
                blocks.append(upper_grads[col_block, row_block])
    full_top = jnp.stack(blocks)
    share_rows = factor_top.shape[1]
    grad_top = lax.dynamic_slice_in_dim(
        full_top, lax.axis_index("pcol") * share_rows, share_rows, 1
    )
    return (grad_low, grad_top)


def solution(mesh):
    in_specs = (
        P(None, "prow", None, None, "pcol", None),
        P(None, "prow", "pcol", None, None, None),
        P(None, "prow", "pcol", None, None, None),
        P(None, "pcol", None),
        P(None, "pcol", None),
        P(None, "pcol", None),
    )
    out_specs = (P(None, "prow", "pcol", None, None, None), P(None, "pcol", None))
    return jax.shard_map(
        per_device, mesh=mesh, in_specs=in_specs, out_specs=out_specs, check_vma=False
    )
```

profile of v0, /device:TPU:7, one launch (start us, length us, event | category | flops | bytes accessed | tf_op | source)
XLA Modules:
  0.0 1293.1 jit_solution(6312719842912323253)
XLA Ops:
  9.0 38.3 %all-gather.3 = f32[2,256,256]{2,1,0:T(8,128)S(1)} all-gather(f32[2,8,256]{2,1,0:T(8,128)S(1)} %get-tuple-element.15), channel_id=5, replica_groups=mesh['prow'=16,'pcol'=32] {'pcol'}, dimensions={1}, use_global_device_ids=true | all-gather | bytes 540672 | tf_op jit(solution)/shard_map/all_gather | solution.py:46
  47.3 28.5 %all-gather.2 = f32[2,256,256]{2,1,0:T(8,128)S(1)} all-gather(f32[2,8,256]{2,1,0:T(8,128)S(1)} %get-tuple-element.16), channel_id=4, replica_groups=mesh['prow'=16,'pcol'=32] {'pcol'}, dimensions={1}, use_global_device_ids=true | all-gather | bytes 540672 | tf_op jit(solution)/shard_map/all_gather | solution.py:46
  77.2 29.8 %all-gather.1 = f32[2,256,256]{2,1,0:T(8,128)S(1)} all-gather(f32[2,8,256]{2,1,0:T(8,128)S(1)} %get-tuple-element.17), channel_id=3, replica_groups=mesh['prow'=16,'pcol'=32] {'pcol'}, dimensions={1}, use_global_device_ids=true | all-gather | bytes 540672 | tf_op jit(solution)/shard_map/all_gather | solution.py:46
  107.8 28.5 %all-gather = f32[2,256,256]{2,1,0:T(8,128)S(1)} all-gather(f32[2,8,256]{2,1,0:T(8,128)S(1)} %get-tuple-element.14), channel_id=2, replica_groups=mesh['prow'=16,'pcol'=32] {'pcol'}, dimensions={1}, use_global_device_ids=true | all-gather | bytes 540672 | tf_op jit(solution)/shard_map/all_gather | solution.py:46
  137.7 111.1 %all-reduce.7.cloned.1.call-done = (f32[256,256]{1,0:T(8,128)}, f32[256,256]{1,0:T(8,128)}, f32[256,256]{1,0:T(8,128)}, f32[256,256]{1,0:T(8,128)}) async-done(((f32[256,256]{1,0:T(8,128)}, f32[256,256]{1,0:T(8,128)}, f32[256,256]{1,0:T(8,128)}, f32[256,256]{1,0:T(8,128)}), (f32[256,256]{1,0:T(8,128)}, f32[256,256]{1,0:T(8,128)}, f32[256,256]{1,0:T(8,128)}, ...) | async-done | bytes 1048592 | tf_op jit(solution)/shard_map/psum | solution.py:15
  248.9 1.7 convolution_bitcast_fusion
  250.5 1.1 copy.31
  252.4 1.2 copy.29
  255.1 1.1 copy.27
  257.0 1.1 copy.25
  259.1 99.2 %reduce-scatter.11.cloned.1.call-done = f32[16,256]{1,0:T(8,128)} async-done(((f32[512,256]{1,0:T(8,128)}), f32[16,256]{1,0:T(8,128)}) %reduce-scatter.11.cloned.1.call-update) | async-done | bytes 16400 | tf_op jit(solution)/shard_map/reduce_scatter | solution.py:54
  358.3 1.2 fusion.67
  361.2 1.0 pad_maximum_fusion
  362.2 103.6 %reduce-scatter.9.cloned.1.call-done = f32[16,256]{1,0:T(8,128)} async-done(((f32[512,256]{1,0:T(8,128)}), f32[16,256]{1,0:T(8,128)}) %reduce-scatter.9.cloned.1.call-update) | async-done | bytes 16400 | tf_op jit(solution)/shard_map/reduce_scatter | solution.py:54
  465.9 76.0 %all-gather.10.cloned.1.call-done = f32[10,256,256]{2,1,0:T(8,128)} async-done(((f32[10,8,256]{2,1,0:T(8,128)}), f32[10,256,256]{2,1,0:T(8,128)}) %all-gather.10.cloned.1.call-update) | async-done | bytes 2621456 | tf_op jit(solution)/shard_map/all_gather | solution.py:91
  541.9 1.3 convolution_subtract_fusion.19
  543.2 1.1 fusion.70
  545.7 99.9 %reduce-scatter.7.cloned.1.call-done = f32[16,256]{1,0:T(8,128)} async-done(((f32[512,256]{1,0:T(8,128)}), f32[16,256]{1,0:T(8,128)}) %reduce-scatter.7.cloned.1.call-update) | async-done | bytes 16400 | tf_op jit(solution)/shard_map/reduce_scatter | solution.py:54
  645.6 1.2 convolution_subtract_fusion.18
  646.8 1.2 convolution_subtract_fusion.17
  648.0 1.1 fusion.74
  649.1 1.1 convolution_bitcast_fusion.11
  650.3 1.1 convolution_bitcast_fusion.12
  651.4 102.5 %reduce-scatter.5.cloned.1.call-done = f32[16,256]{1,0:T(8,128)} async-done(((f32[512,256]{1,0:T(8,128)}), f32[16,256]{1,0:T(8,128)}) %reduce-scatter.5.cloned.1.call-update) | async-done | bytes 16400 | tf_op jit(solution)/shard_map/reduce_scatter | solution.py:54
  755.3 1.2 fusion.79
  756.6 1.1 convolution_bitcast_fusion.13
  757.7 1.9 pad_maximum_fusion.2
  759.6 1.0 pad_maximum_fusion.1
  761.5 68.5 %all-gather.12.cloned.1.call-done = f32[10,256,256]{2,1,0:T(8,128)} async-done(((f32[10,8,256]{2,1,0:T(8,128)}), f32[10,256,256]{2,1,0:T(8,128)}) %all-gather.12.cloned.1.call-update) | async-done | bytes 2621456 | tf_op jit(solution)/shard_map/all_gather | solution.py:92
  829.9 415.0 %all-reduce.5.cloned.1.call-done = (f32[2,256,256]{2,1,0:T(8,128)}, f32[3,256,256]{2,1,0:T(8,128)}, f32[4,256,256]{2,1,0:T(8,128)}, f32[1,256,256]{2,1,0:T(8,128)}) async-done(((f32[2,256,256]{2,1,0:T(8,128)}, f32[3,256,256]{2,1,0:T(8,128)}, f32[4,256,256]{2,1,0:T(8,128)}, f32[1,256,256]{2,1,0:T(8,128)}), (f32[2,256,256]{2,1,0:T(8,128)}, f32[3,256,256]{2,1,0:T(8,128)}, f32[4,256,256]{2,1,0:T(8,128)}, ...) | async-done | bytes 2621456 | tf_op jit(solution)/shard_map/psum | solution.py:139
  1244.9 1.5 fusion.18
  1246.4 1.3 fusion.62
  1247.8 1.5 fusion.66
  1249.5 1.5 fusion.8
  1251.0 1.3 fusion.69
  1252.4 1.6 fusion.7
  1256.4 1.5 fusion.5
  1258.3 1.3 fusion.72
  1259.7 1.5 fusion.6
  1263.1 1.6 convolution_subtract_fusion.11
  1266.2 1.3 fusion.71
  1267.5 1.8 copy.38
  1269.3 1.5 fusion.1
  1270.8 1.5 fusion.2
  1275.0 1.4 fusion.3
  1278.1 1.6 convolution_subtract_fusion.6
  1282.7 1.0 bitcast_dynamic-update-slice_fusion.8
  1283.7 1.1 bitcast_dynamic-update-slice_fusion.7
  (138 shorter events, 27.5 us)
Async XLA Ops:
  8.0 240.9 %all-reduce.7.cloned.1.call-start = ((), (), s32[]{:S(2)}) async-start(), calls=%async_computation.12 | async-start | bytes 2097152 | tf_op jit(solution)/shard_map/psum | solution.py:15
  9.0 128.7 %copy-start.19 = (f32[2,1,256,1,1,256]{5,4,3,2,1,0:T(1,128)S(1)}, f32[2,1,256,1,1,256]{5,4,3,2,1,0:T(1,128)}, u32[]{:S(2)}) copy-start(f32[2,1,256,1,1,256]{5,4,3,2,1,0:T(1,128)} %param.6) | copy-start | bytes 1572868
  137.1 122.0 %all-gather.8.cloned.1.call-start = ((), (), s32[]{:S(2)}) async-start(), calls=%async_computation.8 | async-start | bytes 1081344 | tf_op jit(solution)/shard_map/all_gather | solution.py:93
  137.6 220.7 %reduce-scatter.11.cloned.1.call-start = ((), (), s32[]{:S(2)}) async-start(), calls=%async_computation.7 | async-start | bytes 540672 | tf_op jit(solution)/shard_map/reduce_scatter | solution.py:54
  248.9 2.9 copy-start.25
  248.9 5.5 copy-start.24
  251.7 214.2 %reduce-scatter.9.cloned.1.call-start = ((), (), s32[]{:S(2)}) async-start(), calls=%async_computation.6 | async-start | bytes 540672 | tf_op jit(solution)/shard_map/reduce_scatter | solution.py:54
  251.7 4.6 copy-start.23
  253.6 288.3 %all-gather.10.cloned.1.call-start = ((), (), s32[]{:S(2)}) async-start(), calls=%async_computation.9 | async-start | bytes 2703360 | tf_op jit(solution)/shard_map/all_gather | solution.py:91
  254.3 391.2 %reduce-scatter.7.cloned.1.call-start = ((), (), s32[]{:S(2)}) async-start(), calls=%async_computation.5 | async-start | bytes 540672 | tf_op jit(solution)/shard_map/reduce_scatter | solution.py:54
  254.4 4.6 copy-start.27
  255.1 3.9 copy-start.26
  256.2 497.7 %reduce-scatter.5.cloned.1.call-start = ((), (), s32[]{:S(2)}) async-start(), calls=%async_computation.4 | async-start | bytes 540672 | tf_op jit(solution)/shard_map/reduce_scatter | solution.py:54
  258.1 571.8 %all-gather.12.cloned.1.call-start = ((), (), s32[]{:S(2)}) async-start(), calls=%async_computation.10 | async-start | bytes 2703360 | tf_op jit(solution)/shard_map/all_gather | solution.py:92
  258.7 986.2 %all-reduce.5.cloned.1.call-start = ((), (), s32[]{:S(2)}) async-start(), calls=%async_computation.11 | async-start | bytes 5242880 | tf_op jit(solution)/shard_map/psum | solution.py:139
  541.9 212.1 %copy-start = (f32[10,256,256]{2,1,0:T(8,128)S(1)}, f32[10,256,256]{2,1,0:T(8,128)}, u32[]{:S(2)}) copy-start(f32[10,256,256]{2,1,0:T(8,128)} %all-gather.10.cloned.1.call-done) | copy-start | bytes 7864324
  1249.5 5.0 copy-start.1
  1256.4 3.3 copy-start.11
  1256.4 5.4 copy-start.2
  1257.9 5.2 copy-start.20
  1259.7 5.6 copy-start.7
  1262.4 0.7 copy-start.4
  1269.3 3.1 copy-start.8
  1269.3 3.9 copy-start.3
  1269.3 4.3 copy-start.5
  1272.8 2.2 copy-start.10
  1272.8 2.2 copy-start.16
  1272.8 2.2 copy-start.21
  1273.6 6.8 copy-start.14
  1274.6 3.5 copy-start.22
  1275.0 4.7 copy-start.17
  1278.1 3.9 copy-start.13
  1281.5 3.3 copy-start.18
  1281.5 3.3 copy-start.6
  1281.5 3.3 copy-start.12
  1281.9 3.0 copy-start.15
  1282.6 2.4 copy-start.9
Sparse Core Ops, SparseCore 0:
  137.2 111.6 all-reduce.6
  760.8 484.0 all-reduce.4
Sparse Core Ops, SparseCore 1:
  139.7 67.5 all-gather.7
  251.8 106.5 reduce-scatter.10
  361.2 104.6 reduce-scatter.8
  468.0 73.8 all-gather.9
  544.7 100.8 reduce-scatter.6
  648.6 105.3 reduce-scatter.4
  756.0 73.9 all-gather.11
where the time goes:
time: 1300 us; the launch traced here: 1290 us
  waiting for transfers between devices  1080 us (83%)
  blocking collectives  125 us (10%)
  matrix products  53.2 us (4%)
  between operations  16.7 us (1%)
    psum x1, waiting for transfers between devices, per_device(): summed = lax.psum(local_gram, ('prow', 'pcol'))  415 us
    reduce_scatter x4, waiting for transfers between devices, reduce_one(): lax.psum_scatter(term(jnp.int32(0), lax.axis_size('pcol') * count), 'pcol...  405 us
    all_gather x4, blocking collectives, rows_one(): return lax.all_gather(piece, 'pcol', axis=1, tiled=True)  125 us
    psum x1, waiting for transfers between devices, from_root(): return lax.psum(jnp.where(mine, array, jnp.zeros_like(array)), axis)  111 us
    all_gather x1, waiting for transfers between devices, per_device(): lax.all_gather(factor_top, 'pcol', axis=1, tiled=True)  76 us
    all_gather x1, waiting for transfers between devices, per_device(): lax.all_gather(adjoint_top, 'pcol', axis=1, tiled=True)  68.5 us
    dot_general x30, matrix products, matmul(): jnp.dot(left, right, precision=HIGHEST, preferred_element_type=jnp.float32)  27.1 us
  transfers between devices with their start and end apart: 9, of which 8 were waited for; matrix products, arithmetic and copies ran while one was open for 2% of the time, Pallas kernels for 0%

commit v1 on v0

v1 whole, which is shorter than its diff:
```python
import jax
import jax.numpy as jnp
from jax import lax
from jax.experimental import pallas as pl
from jax.experimental.pallas import tpu as pltpu
from jax.sharding import PartitionSpec as P

NB = 256
K = 4
NBLK = 10
NTOP = NBLK + K
PROWS = 16
PCOLS = 32
CHIPS = 16

HIGHEST = lax.Precision.HIGHEST
MESH = pl.DeviceIdType.MESH
F32 = jnp.float32


def matmul(left, right):
    return jnp.dot(left, right, precision=HIGHEST, preferred_element_type=F32)


def inner_product(left, right):
    return lax.dot_general(
        left, right, (((0,), (0,)), ((), ())), precision=HIGHEST, preferred_element_type=F32
    )


def block_slot(row_block, col_block):
    return row_block * (row_block + 1) // 2 + col_block


def loop(low, high, body):
    lax.fori_loop(low, high, lambda i, carry: (body(i), carry)[1], 0)


def remote(src, dst, send, recv, row, col):
    return pltpu.make_async_remote_copy(
        src_ref=src, dst_ref=dst, send_sem=send, recv_sem=recv, device_id=(row, col), device_id_type=MESH
    )


class Spread:
    def __init__(self, buf, count, sems, place):
        self.buf, self.count, self.place = buf, count, place
        self.line_send, self.line_recv, self.flat_send, self.flat_recv, self.twin_send, self.twin_recv = sems

    def line_copy(self, step, origin):
        p, z, c = self.place
        tile = self.buf.at[p, origin, c]
        peer = lax.rem(z + step, CHIPS) * 2 + c
        return remote(tile, tile, self.line_send.at[step], self.line_recv.at[origin], p, peer)

    def flat_copy(self, step, block):
        p, z, c = self.place
        half = self.buf.at[block, :, c]
        return remote(
            half, half, self.flat_send.at[step], self.flat_recv.at[block], lax.rem(p + step, PROWS), z * 2 + c
        )

    def twin_copy(self, block, core):
        p, z, c = self.place
        half = self.buf.at[block, :, core]
        return remote(half, half, self.twin_send.at[block], self.twin_recv.at[block], p, z * 2 + 1 - c)

    def start_line(self):
        p, z, c = self.place

        @pl.when(p < self.count)
        def _():
            loop(1, CHIPS, lambda step: self.line_copy(step, z).start())

    def start_flat(self):
        p, z, c = self.place

        @pl.when(p < self.count)
        def _():
            loop(1, CHIPS, lambda step: self.line_copy(step, lax.rem(z + step, CHIPS)).wait_recv())
            loop(1, PROWS, lambda step: self.flat_copy(step, p).start())
            self.twin_copy(p, c).start()

    def forward(self):
        p, z, c = self.place

        def body(block):
            @pl.when(block != p)
            def _():
                self.flat_copy(1, block).wait_recv()
                self.twin_copy(block, c).start()

        loop(0, self.count, body)

    def finish(self):
        p, z, c = self.place
        loop(0, self.count, lambda block: self.twin_copy(block, 1 - c).wait_recv())

    def drain(self):
        p, z, c = self.place

        @pl.when(p < self.count)
        def _():
            loop(1, CHIPS, lambda step: self.line_copy(step, z).wait_send())
            loop(1, PROWS, lambda step: self.flat_copy(step, p).wait_send())

        loop(0, self.count, lambda block: self.twin_copy(block, c).wait_send())


def spread_sems(count):
    dma = pltpu.SemaphoreType.DMA
    return [dma((CHIPS,)), dma((CHIPS,)), dma((PROWS,)), dma((count,)), dma((count,)), dma((count,))]


def exchange_kernel(
    trail, factor, adjoint, top_factor, top_adjoint, inverse, low_out, known_out, open_out,
    gathered, partial, pieces, moved, solved, slices, corner, tiles, columns, sums, terms, home,
    ring_send, ring_recv, twin_send, twin_recv, moved_send, moved_recv, sum_send, sum_recv,
    home_send, home_recv, slice_send, slice_recv, tile_send, tile_recv, term_send, term_recv, *spreads
):
    p, q = lax.axis_index("prow"), lax.axis_index("pcol")
    z, c = q // 2, lax.rem(q, 2)
    place = (p, z, c)
    known = Spread(known_out, NTOP, spreads[:6], place)
    opened = Spread(open_out, NBLK, spreads[6:], place)

    def ring_copy(way, step):
        ahead = way == 0
        origin = lax.rem(z + CHIPS - step if ahead else z + step, CHIPS)
        peer = lax.rem(z + 1 if ahead else z + CHIPS - 1, CHIPS)
        part = gathered.at[:, origin * 2 + c]
        return part, peer * 2 + c, origin

    def ring_start(way, step):
        part, peer, _ = ring_copy(way, step)
        remote(part, part, ring_send.at[way, step], ring_recv.at[way, step], p, peer).start()

    def ring_wait(way, step):
        part, peer, origin = ring_copy(way, step)
        remote(part, part, ring_send.at[way, step - 1], ring_recv.at[way, step - 1], p, peer).wait_recv()
        return origin

    def ring_drain(way, step):
        part, peer, _ = ring_copy(way, step)
        remote(part, part, ring_send.at[way, step], ring_recv.at[way, step], p, peer).wait_send()

    def twin_copy(origin, core):
        part = gathered.at[:, origin * 2 + core]
        return remote(part, part, twin_send.at[origin], twin_recv.at[origin], p, z * 2 + 1 - c)

    gathered[:, pl.ds(q, 1)] = factor[...][:, None]
    ring_start(0, 0)
    ring_start(1, 0)
    twin_copy(z, c).start()

    @pl.when(p < NBLK)
    def _():
        known_out[pl.ds(p, 1), pl.ds(z, 1), pl.ds(c, 1)] = top_factor[pl.ds(lax.rem(p, NBLK), 1)][:, None, None]

    @pl.when((p >= NBLK) & (p < NTOP))
    def _():
        known_out[pl.ds(p, 1), pl.ds(z, 1), pl.ds(c, 1)] = inverse[pl.ds(lax.rem(p + 2, K), 1)][:, None, None]

    known.start_line()

    home_row, home_half = lax.rem(q, PROWS), q // PROWS

    def here_or_there(src, dst, send, recv, row, col, act):
        own = (row == p) & (col == q)

        @pl.when(own)
        def _():
            act(pltpu.make_async_copy(src, dst, recv), True)

        @pl.when(jnp.logical_not(own))
        def _():
            act(remote(src, dst, send, recv, row, col), False)

    def move_out(half, act):
        here_or_there(
            adjoint.at[half], moved.at[c], moved_send.at[half], moved_recv.at[c], z, half * PROWS + p, act
        )

    def start(copy, local):
        copy.start()

    def sent(copy, local):
        if not local:
            copy.wait_send()

    def arrived(copy, local):
        copy.wait() if local else copy.wait_recv()

    for half in range(2):
        move_out(half, start)

    def ring_step(step):
        origin = ring_wait(0, step)

        @pl.when(step < CHIPS // 2)
        def _():
            ring_start(0, step)

        twin_copy(origin, c).start()

        @pl.when(step < CHIPS // 2)
        def _():
            other = ring_wait(1, step)

            @pl.when(step < CHIPS // 2 - 1)
            def _():
                ring_start(1, step)

            twin_copy(other, c).start()

    loop(1, 5, ring_step)
    known.start_flat()
    loop(5, CHIPS // 2 + 1, ring_step)
    loop(0, CHIPS, lambda origin: twin_copy(origin, 1 - c).wait_recv())

    everything = gathered[...].reshape(2, NB, K * NB)
    image = inner_product(trail[0], everything[0]) + inner_product(trail[1], everything[1])
    partial[...] = image.reshape(PROWS, 16, K * NB)

    def sum_copy(step, source):
        target = lax.rem(p + step, PROWS)
        return remote(partial.at[target], pieces.at[source], sum_send.at[step], sum_recv.at[source], target, q)

    loop(1, PROWS, lambda step: sum_copy(step, p).start())
    pieces[pl.ds(p, 1)] = partial[pl.ds(p, 1)]

    known.forward()
    known.finish()
    for half in range(2):
        here_or_there(
            adjoint.at[0], moved.at[half], moved_send.at[0], moved_recv.at[half], home_row, 2 * p + half, arrived
        )

    loop(1, PROWS, lambda step: sum_copy(step, lax.rem(p + step, PROWS)).wait_recv())
    total = pieces[0]
    for source in range(1, PROWS):
        total = total + pieces[source]
    residual = moved[...].reshape(16, K * NB) - 2.0 * total

    def block(slot):
        return known_out[slot].reshape(NB, NB)

    parts = [residual[:, j * NB : (j + 1) * NB] for j in range(K)]
    for j in reversed(range(K)):
        parts[j] = matmul(parts[j], block(NBLK + j))
        for earlier in range(j):
            parts[earlier] = parts[earlier] - matmul(parts[j], block(block_slot(j, earlier)))
        solved[:, :, j * NB : (j + 1) * NB] = parts[j].reshape(2, 8, NB)
        for side in range(2):
            slices[2 * j + side] = parts[j][:, side * 128 : (side + 1) * 128]

    base, spot = (p // 8) * 8, lax.rem(p, 8)

    def slice_copy(step, source):
        target = lax.rem(spot + step, 8)
        return remote(slices.at[target], corner.at[source], slice_send.at[step], slice_recv.at[source], base + target, q)

    loop(1, 8, lambda step: slice_copy(step, spot).start())
    corner[pl.ds(spot, 1)] = slices[pl.ds(spot, 1)]

    def home_out(half, act):
        here_or_there(
            solved.at[half], home.at[home_half], home_send.at[half], home_recv.at[home_half],
            home_row, 2 * p + half, act,
        )

    for half in range(2):
        home_out(half, start)
    loop(1, 8, lambda step: slice_copy(step, lax.rem(spot + step, 8)).wait_recv())
    tiles[...] = corner[...].reshape(128, 128).T.reshape(16, 8, 128)

    panel, upper = spot // 2, lax.rem(spot, 2)
    quarter = home_half * 2 + p // 8

    def tile_out(k, act):
        here_or_there(
            tiles.at[k], columns.at[panel, quarter], tile_send.at[k], tile_recv.at[panel, quarter],
            home_row, upper * 16 + k, act,
        )

    loop(0, 16, lambda k: tile_out(k, start))

    def tile_in(index):
        j, part = index // 4, lax.rem(index, 4)
        source_row = lax.rem(part, 2) * 8 + 2 * j + home_half
        source_col = (part // 2) * PROWS + p
        here_or_there(
            tiles.at[0], columns.at[j, part], tile_send.at[0], tile_recv.at[j, part], source_row, source_col, arrived
        )

    loop(0, 16, tile_in)
    wide = jnp.concatenate([columns[:, part].reshape(32, 128) for part in range(4)], axis=1)
    gram = matmul(wide, gathered[...].reshape(2 * NB, K * NB))
    for j in range(K):
        for i in range(j + 1):
            terms[block_slot(j, i)] = gram[j * 8 : (j + 1) * 8, i * NB : (i + 1) * NB]

    def term_copy(target, source):
        return remote(terms.at[target], sums.at[source], term_send.at[target], term_recv.at[source], target, q)

    def each_term(act):
        def body(target):
            @pl.when(target != p)
            def _():
                act(term_copy(target, p))

        loop(0, NBLK, body)

    each_term(lambda copy: copy.start())

    @pl.when(p < NBLK)
    def _():
        own = lax.rem(p, NBLK)
        sums[pl.ds(p, 1)] = terms[pl.ds(own, 1)]

        def body(step):
            source = lax.rem(p + step, PROWS)
            term_copy(own, source).wait_recv()

        loop(1, PROWS, body)
        whole = sums[0]
        for source in range(1, PROWS):
            whole = whole + sums[source]
        open_out[pl.ds(p, 1), pl.ds(z, 1), pl.ds(c, 1)] = (top_adjoint[own] - whole)[None, None, None]

    opened.start_line()
    opened.start_flat()
    for half in range(2):
        here_or_there(
            solved.at[0], home.at[half], home_send.at[0], home_recv.at[half], z, half * PROWS + p, arrived
        )
    low_out[...] = home[...]
    opened.forward()
    opened.finish()

    for way in range(2):
        loop(0, CHIPS // 2 - way, lambda step: ring_drain(way, step))
    loop(0, CHIPS, lambda origin: twin_copy(origin, c).wait_send())
    for half in range(2):
        move_out(half, sent)
        home_out(half, sent)
    loop(1, PROWS, lambda step: sum_copy(step, p).wait_send())
    loop(1, 8, lambda step: slice_copy(step, spot).wait_send())
    loop(0, 16, lambda k: tile_out(k, sent))
    each_term(lambda copy: copy.wait_send())
    known.drain()
    opened.drain()


def half_lower(square):
    row_ids = lax.broadcasted_iota(jnp.int32, (NB, NB), 0)
    col_ids = lax.broadcasted_iota(jnp.int32, (NB, NB), 1)
    return jnp.where(row_ids > col_ids, square, jnp.where(row_ids == col_ids, 0.5 * square, 0.0))


def lower(square):
    row_ids = lax.broadcasted_iota(jnp.int32, (NB, NB), 0)
    col_ids = lax.broadcasted_iota(jnp.int32, (NB, NB), 1)
    return jnp.where(row_ids >= col_ids, square, 0.0)


def top_kernel(known, opened, out, full):
    def factor(r, j):
        return known[block_slot(r, j)].reshape(NB, NB)

    def inverse(j):
        return known[NBLK + j].reshape(NB, NB)

    def grad(r, j):
        return full[block_slot(r, j)]

    for j in reversed(range(K)):
        for r in range(j + 1, K):
            rest = opened[block_slot(r, j)].reshape(NB, NB) - 2.0 * matmul(grad(r, r), factor(r, j))
            for middle in range(j + 1, r):
                rest = rest - matmul(grad(r, middle), factor(middle, j))
            for beyond in range(r + 1, K):
                rest = rest - inner_product(grad(beyond, r), factor(beyond, j))
            full[block_slot(r, j)] = matmul(rest, inverse(j))
        adj = opened[block_slot(j, j)].reshape(NB, NB)
        for r in range(j + 1, K):
            adj = adj - inner_product(grad(r, j), factor(r, j))
        inner = half_lower(inner_product(lower(factor(j, j)), lower(adj)))
        spread = inner_product(inverse(j), matmul(inner, inverse(j)))
        full[block_slot(j, j)] = 0.5 * (spread + spread.T)
    rows = pl.ds(pl.multiple_of(lax.axis_index("pcol") * 8, 8), 8)
    out[...] = full[:, rows, :]


def per_device(adjoint_trail, factor_low, adjoint_low, factor_top, adjoint_top, diag_inverse):
    dma = pltpu.SemaphoreType.DMA
    vmem = pl.BlockSpec(memory_space=pltpu.VMEM)
    wide = K * NB
    low_grad, known, opened = pl.pallas_call(
        exchange_kernel,
        out_shape=[
            jax.ShapeDtypeStruct((2, 8, wide), F32),
            jax.ShapeDtypeStruct((NTOP, CHIPS, 2, 8, NB), F32),
            jax.ShapeDtypeStruct((NBLK, CHIPS, 2, 8, NB), F32),
        ],
        in_specs=[vmem] * 6,
        out_specs=[vmem] * 3,
        scratch_shapes=[
            pltpu.VMEM((2, PCOLS, 8, wide), F32),
            pltpu.VMEM((PROWS, 16, wide), F32),
            pltpu.VMEM((PROWS, 16, wide), F32),
            pltpu.VMEM((2, 8, wide), F32),
            pltpu.VMEM((2, 8, wide), F32),
            pltpu.VMEM((8, 16, 128), F32),
            pltpu.VMEM((8, 16, 128), F32),
            pltpu.VMEM((16, 8, 128), F32),
            pltpu.VMEM((4, 4, 8, 128), F32),
            pltpu.VMEM((PROWS, 8, NB), F32),
            pltpu.VMEM((NBLK, 8, NB), F32),
            pltpu.VMEM((2, 8, wide), F32),
            dma((2, 8)), dma((2, 8)), dma((CHIPS,)), dma((CHIPS,)), dma((2,)), dma((2,)),
            dma((PROWS,)), dma((PROWS,)), dma((2,)), dma((2,)), dma((8,)), dma((8,)),
            dma((16,)), dma((4, 4)), dma((NBLK,)), dma((PROWS,)),
            *spread_sems(NTOP),
            *spread_sems(NBLK),
        ],
        compiler_params=pltpu.CompilerParams(has_side_effects=True, vmem_limit_bytes=40 * 1024 * 1024),
        name="exchange",
    )(
        adjoint_trail.reshape(2, NB, NB),
        factor_low.reshape(2, 8, wide),
        adjoint_low.reshape(2, 8, wide),
        factor_top,
        adjoint_top,
        diag_inverse,
    )
    grad_top = pl.pallas_call(
        top_kernel,
        out_shape=jax.ShapeDtypeStruct((NBLK, 8, NB), F32),
        in_specs=[vmem] * 2,
        out_specs=vmem,
        scratch_shapes=[pltpu.VMEM((NBLK, NB, NB), F32)],
        compiler_params=pltpu.CompilerParams(vmem_limit_bytes=40 * 1024 * 1024),
        name="top",
    )(known, opened)
    return low_grad.reshape(factor_low.shape), grad_top


def solution(mesh):
    in_specs = (
        P(None, "prow", None, None, "pcol", None),
        P(None, "prow", "pcol", None, None, None),
        P(None, "prow", "pcol", None, None, None),
        P(None, "pcol", None),
        P(None, "pcol", None),
        P(None, "pcol", None),
    )
    out_specs = (P(None, "prow", "pcol", None, None, None), P(None, "pcol", None))
    return jax.shard_map(
        per_device, mesh=mesh, in_specs=in_specs, out_specs=out_specs, check_vma=False
    )
```

time: 1300 us -> 189 us (0.15)
  the two profiles are of different devices: /device:TPU:7 before, /device:TPU:25 now
where the time goes in v1:
time: 189 us
  Pallas kernels  182 us (96%)
  local copies, waits for them, and re-layouts  6.01 us (3%)
    pallas_call x1, Pallas kernels, per_device(): pl.pallas_call(exchange_kernel, out_shape=[jax.ShapeDtypeStruct((2, 8, wi...  167 us
    pallas_call x1, Pallas kernels, per_device(): pl.pallas_call(top_kernel, out_shape=jax.ShapeDtypeStruct((NBLK, 8, NB),...  14.9 us
    unnamed x8, local copies, waits for them, and re-layouts  4.26 us

profile of v1, /device:TPU:25, one launch (start us, length us, event | category | flops | bytes accessed | tf_op | source)
XLA Modules:
  0.0 188.9 jit_solution(8492076058035397092)
XLA Ops:
  0.6 0.9 reshape.17.factor
  1.5 0.9 reshape.18.adjoint
  2.4 1.1 copy.11
  3.5 0.0 copy-start
  3.5 0.9 copy-done
  4.4 0.0 copy-start.1
  4.4 0.9 copy-done.1
  5.2 0.0 copy-start.2
  5.2 0.8 copy-done.2
  6.0 167.3 %exchange.1 = (f32[2,8,1024]{2,1,0:T(8,128)S(1)}, f32[14,16,2,8,256]{4,3,2,1,0:T(8,128)S(1)}, f32[10,16,2,8,256]{4,3,2,1,0:T(8,128)S(1)}) custom-call(f32[2,256,256]{2,1,0:T(8,128)S(1)} %bitcast.4, f32[2,8,1024]{2,1,0:T(8,128)S(1)} %reshape.17.factor, f32[2,8,1024]{2,1,0:T(8,128)S(1)} %reshape.18.adjoint, f32[10,8,256]{2,1,0:T(8,128)S(1)} %copy-done, ...), custom_call_target="tpu_custom_call" | custom-call | tf_op jit(solution)/shard_map/exchange/pallas_call | solution.py:399
  173.3 0.7 copy.8
  174.0 14.9 %top.1 = f32[10,8,256]{2,1,0:T(8,128)} custom-call(f32[14,16,2,8,256]{4,3,2,1,0:T(8,128)S(1)} %get-tuple-element.6.known, f32[10,16,2,8,256]{4,3,2,1,0:T(8,128)S(1)} %get-tuple-element.7.opened), custom_call_target="tpu_custom_call" | custom-call | tf_op jit(solution)/shard_map/top/pallas_call | solution.py:437
Async XLA Ops:
  3.5 0.9 copy-start
  4.4 0.9 copy-start.1
  5.2 0.8 copy-start.2

commit v2 on v1

--- a/solution.py
+++ b/solution.py
@@ -12,6 +12,7 @@
 PROWS = 16
 PCOLS = 32
 CHIPS = 16
+SIDE = 4
 
 HIGHEST = lax.Precision.HIGHEST
 MESH = pl.DeviceIdType.MESH
@@ -45,7 +46,7 @@
 class Spread:
     def __init__(self, buf, count, sems, place):
         self.buf, self.count, self.place = buf, count, place
-        self.line_send, self.line_recv, self.flat_send, self.flat_recv, self.twin_send, self.twin_recv = sems
+        self.line_send, self.line_recv, self.near_send, self.far_send, self.flat_recv, self.twin_send, self.twin_recv = sems
 
     def line_copy(self, step, origin):
         p, z, c = self.place
@@ -53,11 +54,23 @@
         peer = lax.rem(z + step, CHIPS) * 2 + c
         return remote(tile, tile, self.line_send.at[step], self.line_recv.at[origin], p, peer)
 
-    def flat_copy(self, step, block):
+    def peers(self, step):
+        p, z, c = self.place
+        x, y = p // SIDE, lax.rem(p, SIDE)
+        along_x = lax.rem(x + step, SIDE) * SIDE + y
+        along_y = x * SIDE + lax.rem(y + step, SIDE)
+        return along_x * (1 - c) + along_y * c, along_y * (1 - c) + along_x * c
+
+    def near_copy(self, step):
+        p, z, c = self.place
+        half = self.buf.at[p, :, c]
+        return remote(half, half, self.near_send.at[step], self.flat_recv.at[p], self.peers(step)[0], z * 2 + c)
+
+    def far_copy(self, block, origin, step):
         p, z, c = self.place
         half = self.buf.at[block, :, c]
         return remote(
-            half, half, self.flat_send.at[step], self.flat_recv.at[block], lax.rem(p + step, PROWS), z * 2 + c
+            half, half, self.far_send.at[origin, step], self.flat_recv.at[block], self.peers(step)[1], z * 2 + c
         )
 
     def twin_copy(self, block, core):
@@ -78,23 +91,44 @@
         @pl.when(p < self.count)
         def _():
             loop(1, CHIPS, lambda step: self.line_copy(step, lax.rem(z + step, CHIPS)).wait_recv())
-            loop(1, PROWS, lambda step: self.flat_copy(step, p).start())
+
+            def body(step):
+                self.near_copy(step).start()
+                self.far_copy(p, 0, step).start()
+
+            loop(1, SIDE, body)
             self.twin_copy(p, c).start()
 
-    def forward(self):
-        p, z, c = self.place
-
-        def body(block):
-            @pl.when(block != p)
+    def relay(self):
+        def body(origin):
+            block = self.peers(origin)[0]
+
+            @pl.when(block < self.count)
             def _():
-                self.flat_copy(1, block).wait_recv()
-                self.twin_copy(block, c).start()
-
-        loop(0, self.count, body)
-
-    def finish(self):
-        p, z, c = self.place
-        loop(0, self.count, lambda block: self.twin_copy(block, 1 - c).wait_recv())
+                self.far_copy(block, origin, 1).wait_recv()
+                loop(1, SIDE, lambda step: self.far_copy(block, origin, step).start())
+
+        loop(1, SIDE, body)
+
+    def share(self, block):
+        p, z, c = self.place
+        x, y = p // SIDE, lax.rem(p, SIDE)
+        straight = (block // SIDE) * (1 - c) + lax.rem(block, SIDE) * c
+        mine = x * (1 - c) + y * c
+        cross = lax.rem(block, SIDE) * (1 - c) + (block // SIDE) * c
+        level = y * (1 - c) + x * c
+
+        @pl.when(block != p)
+        def _():
+            @pl.when((straight == mine) | (cross != level))
+            def _():
+                self.far_copy(block, 0, 1).wait_recv()
+
+            self.twin_copy(block, c).start()
+
+    def finish(self, block):
+        p, z, c = self.place
+        self.twin_copy(block, 1 - c).wait_recv()
 
     def drain(self):
         p, z, c = self.place
@@ -102,55 +136,64 @@
         @pl.when(p < self.count)
         def _():
             loop(1, CHIPS, lambda step: self.line_copy(step, z).wait_send())
-            loop(1, PROWS, lambda step: self.flat_copy(step, p).wait_send())
-
+
+            def body(step):
+                self.near_copy(step).wait_send()
+                self.far_copy(p, 0, step).wait_send()
+
+            loop(1, SIDE, body)
+
+        def relayed(origin):
+            block = self.peers(origin)[0]
+
+            @pl.when(block < self.count)
+            def _():
+                loop(1, SIDE, lambda step: self.far_copy(block, origin, step).wait_send())
+
+        loop(1, SIDE, relayed)
         loop(0, self.count, lambda block: self.twin_copy(block, c).wait_send())
 
 
 def spread_sems(count):
     dma = pltpu.SemaphoreType.DMA
-    return [dma((CHIPS,)), dma((CHIPS,)), dma((PROWS,)), dma((count,)), dma((count,)), dma((count,))]
+    return [
+        dma((CHIPS,)), dma((CHIPS,)), dma((SIDE,)), dma((SIDE, SIDE)), dma((PROWS,)), dma((count,)), dma((count,))
+    ]
 
 
 def exchange_kernel(
-    trail, factor, adjoint, top_factor, top_adjoint, inverse, low_out, known_out, open_out,
-    gathered, partial, pieces, moved, solved, slices, corner, tiles, columns, sums, terms, home,
+    trail, factor, adjoint, top_factor, top_adjoint, inverse, low_out, top_out,
+    known_out, open_out, full, gathered, partial, pieces, moved, solved, slices, corner, tiles, columns, sums, terms, home,
     ring_send, ring_recv, twin_send, twin_recv, moved_send, moved_recv, sum_send, sum_recv,
     home_send, home_recv, slice_send, slice_recv, tile_send, tile_recv, term_send, term_recv, *spreads
 ):
     p, q = lax.axis_index("prow"), lax.axis_index("pcol")
     z, c = q // 2, lax.rem(q, 2)
     place = (p, z, c)
-    known = Spread(known_out, NTOP, spreads[:6], place)
-    opened = Spread(open_out, NBLK, spreads[6:], place)
-
-    def ring_copy(way, step):
+    known = Spread(known_out, NTOP, spreads[:7], place)
+    opened = Spread(open_out, NBLK, spreads[7:], place)
+
+    def ring_copy(way, half, step, slot):
         ahead = way == 0
         origin = lax.rem(z + CHIPS - step if ahead else z + step, CHIPS)
         peer = lax.rem(z + 1 if ahead else z + CHIPS - 1, CHIPS)
-        part = gathered.at[:, origin * 2 + c]
-        return part, peer * 2 + c, origin
-
-    def ring_start(way, step):
-        part, peer, _ = ring_copy(way, step)
-        remote(part, part, ring_send.at[way, step], ring_recv.at[way, step], p, peer).start()
-
-    def ring_wait(way, step):
-        part, peer, origin = ring_copy(way, step)
-        remote(part, part, ring_send.at[way, step - 1], ring_recv.at[way, step - 1], p, peer).wait_recv()
-        return origin
-
-    def ring_drain(way, step):
-        part, peer, _ = ring_copy(way, step)
-        remote(part, part, ring_send.at[way, step], ring_recv.at[way, step], p, peer).wait_send()
+        part = gathered.at[half, origin * 2 + c]
+        return remote(part, part, ring_send.at[way, half, slot], ring_recv.at[way, half, slot], p, peer * 2 + c)
+
+    def ring_start(way, half, step):
+        ring_copy(way, half, step, step).start()
+
+    def ring_wait(way, half, step):
+        ring_copy(way, half, step, step - 1).wait_recv()
 
     def twin_copy(origin, core):
         part = gathered.at[:, origin * 2 + core]
         return remote(part, part, twin_send.at[origin], twin_recv.at[origin], p, z * 2 + 1 - c)
 
     gathered[:, pl.ds(q, 1)] = factor[...][:, None]
-    ring_start(0, 0)
-    ring_start(1, 0)
+    for half in range(2):
+        for way in range(2):
+            ring_start(way, half, 0)
     twin_copy(z, c).start()
 
     @pl.when(p < NBLK)
@@ -195,27 +238,29 @@
         move_out(half, start)
 
     def ring_step(step):
-        origin = ring_wait(0, step)
-
-        @pl.when(step < CHIPS // 2)
-        def _():
-            ring_start(0, step)
-
-        twin_copy(origin, c).start()
-
-        @pl.when(step < CHIPS // 2)
-        def _():
-            other = ring_wait(1, step)
+        for half in range(2):
+            ring_wait(0, half, step)
+
+            @pl.when(step < CHIPS // 2)
+            def _():
+                ring_start(0, half, step)
+                ring_wait(1, half, step)
 
             @pl.when(step < CHIPS // 2 - 1)
             def _():
-                ring_start(1, step)
-
-            twin_copy(other, c).start()
-
-    loop(1, 5, ring_step)
+                ring_start(1, half, step)
+
+        twin_copy(lax.rem(z + CHIPS - step, CHIPS), c).start()
+
+        @pl.when(step < CHIPS // 2)
+        def _():
+            twin_copy(lax.rem(z + step, CHIPS), c).start()
+
+    loop(1, 4, ring_step)
     known.start_flat()
-    loop(5, CHIPS // 2 + 1, ring_step)
+    loop(4, 7, ring_step)
+    known.relay()
+    loop(7, CHIPS // 2 + 1, ring_step)
     loop(0, CHIPS, lambda origin: twin_copy(origin, 1 - c).wait_recv())
 
     everything = gathered[...].reshape(2, NB, K * NB)
@@ -229,8 +274,8 @@
     loop(1, PROWS, lambda step: sum_copy(step, p).start())
     pieces[pl.ds(p, 1)] = partial[pl.ds(p, 1)]
 
-    known.forward()
-    known.finish()
+    loop(0, NTOP, known.share)
+    loop(0, NTOP, known.finish)
     for half in range(2):
         here_or_there(
             adjoint.at[0], moved.at[half], moved_send.at[0], moved_recv.at[half], home_row, 2 * p + half, arrived
@@ -330,16 +375,30 @@
 
     opened.start_line()
     opened.start_flat()
+    opened.relay()
+
+    def share_column(j):
+        for r in range(j, K):
+            opened.share(block_slot(r, j))
+
+    share_column(K - 1)
+    share_column(K - 2)
+    for j in reversed(range(K)):
+        for r in range(j, K):
+            opened.finish(block_slot(r, j))
+        top_column(j, known_out, open_out, full)
+        if j >= 2:
+            share_column(j - 2)
+    top_out[...] = full[:, pl.ds(pl.multiple_of(q * 8, 8), 8), :]
     for half in range(2):
         here_or_there(
             solved.at[0], home.at[half], home_send.at[0], home_recv.at[half], z, half * PROWS + p, arrived
         )
     low_out[...] = home[...]
-    opened.forward()
-    opened.finish()
-
-    for way in range(2):
-        loop(0, CHIPS // 2 - way, lambda step: ring_drain(way, step))
+
+    for half in range(2):
+        for way in range(2):
+            loop(0, CHIPS // 2 - way, lambda step: ring_copy(way, half, step, step).wait_send())
     loop(0, CHIPS, lambda origin: twin_copy(origin, c).wait_send())
     for half in range(2):
         move_out(half, sent)
@@ -364,48 +423,45 @@
     return jnp.where(row_ids >= col_ids, square, 0.0)
 
 
-def top_kernel(known, opened, out, full):
+def top_column(j, known, opened, full):
     def factor(r, j):
         return known[block_slot(r, j)].reshape(NB, NB)
 
-    def inverse(j):
-        return known[NBLK + j].reshape(NB, NB)
-
     def grad(r, j):
         return full[block_slot(r, j)]
 
-    for j in reversed(range(K)):
-        for r in range(j + 1, K):
-            rest = opened[block_slot(r, j)].reshape(NB, NB) - 2.0 * matmul(grad(r, r), factor(r, j))
-            for middle in range(j + 1, r):
-                rest = rest - matmul(grad(r, middle), factor(middle, j))
-            for beyond in range(r + 1, K):
-                rest = rest - inner_product(grad(beyond, r), factor(beyond, j))
-            full[block_slot(r, j)] = matmul(rest, inverse(j))
-        adj = opened[block_slot(j, j)].reshape(NB, NB)
-        for r in range(j + 1, K):
-            adj = adj - inner_product(grad(r, j), factor(r, j))
-        inner = half_lower(inner_product(lower(factor(j, j)), lower(adj)))
-        spread = inner_product(inverse(j), matmul(inner, inverse(j)))
-        full[block_slot(j, j)] = 0.5 * (spread + spread.T)
-    rows = pl.ds(pl.multiple_of(lax.axis_index("pcol") * 8, 8), 8)
-    out[...] = full[:, rows, :]
+    inverse = known[NBLK + j].reshape(NB, NB)
+    for r in range(j + 1, K):
+        rest = opened[block_slot(r, j)].reshape(NB, NB) - 2.0 * matmul(grad(r, r), factor(r, j))
+        for middle in range(j + 1, r):
+            rest = rest - matmul(grad(r, middle), factor(middle, j))
+        for beyond in range(r + 1, K):
+            rest = rest - inner_product(grad(beyond, r), factor(beyond, j))
+        full[block_slot(r, j)] = matmul(rest, inverse)
+    adj = opened[block_slot(j, j)].reshape(NB, NB)
+    for r in range(j + 1, K):
+        adj = adj - inner_product(grad(r, j), factor(r, j))
+    inner = half_lower(inner_product(lower(factor(j, j)), lower(adj)))
+    spread = inner_product(inverse, matmul(inner, inverse))
+    full[block_slot(j, j)] = 0.5 * (spread + spread.T)
 
 
 def per_device(adjoint_trail, factor_low, adjoint_low, factor_top, adjoint_top, diag_inverse):
     dma = pltpu.SemaphoreType.DMA
     vmem = pl.BlockSpec(memory_space=pltpu.VMEM)
     wide = K * NB
-    low_grad, known, opened = pl.pallas_call(
+    low_grad, grad_top = pl.pallas_call(
         exchange_kernel,
         out_shape=[
             jax.ShapeDtypeStruct((2, 8, wide), F32),
-            jax.ShapeDtypeStruct((NTOP, CHIPS, 2, 8, NB), F32),
-            jax.ShapeDtypeStruct((NBLK, CHIPS, 2, 8, NB), F32),
+            jax.ShapeDtypeStruct((NBLK, 8, NB), F32),
         ],
         in_specs=[vmem] * 6,
-        out_specs=[vmem] * 3,
+        out_specs=[vmem] * 2,
         scratch_shapes=[
+            pltpu.VMEM((NTOP, CHIPS, 2, 8, NB), F32),
+            pltpu.VMEM((NBLK, CHIPS, 2, 8, NB), F32),
+            pltpu.VMEM((NBLK, NB, NB), F32),
             pltpu.VMEM((2, PCOLS, 8, wide), F32),
             pltpu.VMEM((PROWS, 16, wide), F32),
             pltpu.VMEM((PROWS, 16, wide), F32),
@@ -418,7 +474,7 @@
             pltpu.VMEM((PROWS, 8, NB), F32),
             pltpu.VMEM((NBLK, 8, NB), F32),
             pltpu.VMEM((2, 8, wide), F32),
-            dma((2, 8)), dma((2, 8)), dma((CHIPS,)), dma((CHIPS,)), dma((2,)), dma((2,)),
+            dma((2, 2, 8)), dma((2, 2, 8)), dma((CHIPS,)), dma((CHIPS,)), dma((2,)), dma((2,)),
             dma((PROWS,)), dma((PROWS,)), dma((2,)), dma((2,)), dma((8,)), dma((8,)),
             dma((16,)), dma((4, 4)), dma((NBLK,)), dma((PROWS,)),
             *spread_sems(NTOP),
@@ -434,15 +490,6 @@
         adjoint_top,
         diag_inverse,
     )
-    grad_top = pl.pallas_call(
-        top_kernel,
-        out_shape=jax.ShapeDtypeStruct((NBLK, 8, NB), F32),
-        in_specs=[vmem] * 2,
-        out_specs=vmem,
-        scratch_shapes=[pltpu.VMEM((NBLK, NB, NB), F32)],
-        compiler_params=pltpu.CompilerParams(vmem_limit_bytes=40 * 1024 * 1024),
-        name="top",
-    )(known, opened)
     return low_grad.reshape(factor_low.shape), grad_top
 
 

time: 189 us -> 162 us (0.86)
  the two profiles are of different devices: /device:TPU:25 before, /device:TPU:7 now
where the time goes in v2:
time: 162 us; the launch traced here: 161 us
  Pallas kernels  157 us (97%)
  local copies, waits for them, and re-layouts  3.38 us (2%)
    pallas_call x1, Pallas kernels, per_device(): pl.pallas_call(exchange_kernel, out_shape=[jax.ShapeDtypeStruct((2, 8, wi...  157 us

profile of v2, /device:TPU:7, one launch (start us, length us, event | category | flops | bytes accessed | tf_op | source)
XLA Modules:
  0.0 160.9 jit_solution(9830418704002189244)
XLA Ops:
  0.6 0.0 copy-start.3
  0.6 0.9 reshape.17.factor
  1.5 0.0 copy-done.3
  1.6 0.0 copy-start
  1.6 0.0 copy-start.1
  1.6 0.0 copy-start.2
  1.6 1.1 copy.11
  2.8 0.0 copy-done
  2.8 0.0 copy-done.1
  2.8 0.0 copy-done.2
  2.8 156.8 %exchange.1 = (f32[2,8,1024]{2,1,0:T(8,128)S(1)}, f32[10,8,256]{2,1,0:T(8,128)S(1)}) custom-call(f32[2,256,256]{2,1,0:T(8,128)S(1)} %bitcast.4, f32[2,8,1024]{2,1,0:T(8,128)S(1)} %reshape.17.factor, f32[2,8,1024]{2,1,0:T(8,128)S(1)} %reshape.18.adjoint, f32[10,8,256]{2,1,0:T(8,128)S(1)} %copy-done, f32[10,8,256]{2,1,0:T(8,128)S(1)} %copy-done.1, ...), custom_call_target="tpu_custom_call" | custom-call | tf_op jit(solution)/shard_map/exchange/pallas_call | solution.py:453
  159.6 0.7 copy.8
  160.3 0.6 copy.13
  (1 shorter events, 0.0 us)
Async XLA Ops:
  0.6 0.9 copy-start.3
  1.6 1.2 copy-start
  1.6 1.2 copy-start.1
  1.6 1.2 copy-start.2

commit v3 on v2

--- a/solution.py
+++ b/solution.py
@@ -43,6 +43,12 @@
     )
 
 
+def far_first(index):
+    rest = CHIPS - index
+    odd = lax.rem(rest, 2)
+    return (rest // 2 + 1) * odd + (CHIPS - rest // 2) * (1 - odd)
+
+
 class Spread:
     def __init__(self, buf, count, sems, place):
         self.buf, self.count, self.place = buf, count, place
@@ -83,7 +89,7 @@
 
         @pl.when(p < self.count)
         def _():
-            loop(1, CHIPS, lambda step: self.line_copy(step, z).start())
+            loop(1, CHIPS, lambda index: self.line_copy(far_first(index), z).start())
 
     def start_flat(self):
         p, z, c = self.place
@@ -162,8 +168,8 @@
 
 
 def exchange_kernel(
-    trail, factor, adjoint, top_factor, top_adjoint, inverse, low_out, top_out,
-    known_out, open_out, full, gathered, partial, pieces, moved, solved, slices, corner, tiles, columns, sums, terms, home,
+    trail, factor_in, adjoint_in, factor_top_in, adjoint_top_in, inverse_in, low_out, top_out,
+    factor, adjoint_raw, adjoint, top_factor, top_adjoint, inverse, input_sems, known_out, open_out, full, gathered, partial, pieces, moved, solved, slices, corner, tiles, columns, sums, terms, home,
     ring_send, ring_recv, twin_send, twin_recv, moved_send, moved_recv, sum_send, sum_recv,
     home_send, home_recv, slice_send, slice_recv, tile_send, tile_recv, term_send, term_recv, *spreads
 ):
@@ -173,28 +179,61 @@
     known = Spread(known_out, NTOP, spreads[:7], place)
     opened = Spread(open_out, NBLK, spreads[7:], place)
 
-    def ring_copy(way, half, step, slot):
-        ahead = way == 0
-        origin = lax.rem(z + CHIPS - step if ahead else z + step, CHIPS)
-        peer = lax.rem(z + 1 if ahead else z + CHIPS - 1, CHIPS)
-        part = gathered.at[half, origin * 2 + c]
-        return remote(part, part, ring_send.at[way, half, slot], ring_recv.at[way, half, slot], p, peer * 2 + c)
-
-    def ring_start(way, half, step):
-        ring_copy(way, half, step, step).start()
-
-    def ring_wait(way, half, step):
-        ring_copy(way, half, step, step - 1).wait_recv()
-
-    def twin_copy(origin, core):
-        part = gathered.at[:, origin * 2 + core]
-        return remote(part, part, twin_send.at[origin], twin_recv.at[origin], p, z * 2 + 1 - c)
-
-    gathered[:, pl.ds(q, 1)] = factor[...][:, None]
-    for half in range(2):
-        for way in range(2):
-            ring_start(way, half, 0)
-    twin_copy(z, c).start()
+    home_row, home_half = lax.rem(q, PROWS), q // PROWS
+
+    loads = [
+        pltpu.make_async_copy(src, dst, input_sems.at[i])
+        for i, (src, dst) in enumerate([
+            (factor_in, factor), (factor_top_in, top_factor), (inverse_in, inverse),
+            (adjoint_in, adjoint_raw), (adjoint_top_in, top_adjoint),
+        ])
+    ]
+    for load in loads:
+        load.start()
+
+    barrier = pltpu.get_barrier_semaphore()
+
+    def greet(row, col):
+        @pl.when((row != p) | (col != q))
+        def _():
+            pl.semaphore_signal(barrier, inc=1, device_id=(row, col), device_id_type=MESH)
+
+    loop(1, PROWS, lambda step: greet(lax.rem(p + step, PROWS), q))
+    loop(1, PCOLS, lambda step: greet(p, lax.rem(q + step, PCOLS)))
+    for half in range(2):
+        greet(z, half * PROWS + p)
+        greet(home_row, 2 * p + half)
+    loads[0].wait()
+    for j in range(K):
+        gathered[:, pl.ds(q, 1), :, j * NB : (j + 1) * NB] = factor[:, :, j][:, None]
+    own = 1 // (1 + (z - p) * (z - p) + (home_row - p) * (home_row - p))
+    pl.semaphore_wait(barrier, PROWS + PCOLS + 2 - 2 * own)
+
+    steps = CHIPS // 2 - c
+
+    def origin_of(step, core):
+        return lax.rem(z + (CHIPS - step) * (1 - core) + step * core, CHIPS)
+
+    def ring_copy(half, core, step, slot):
+        part = gathered.at[half, origin_of(step, c) * 2 + core]
+        peer = lax.rem(z + 1 + (CHIPS - 2) * c, CHIPS)
+        return remote(
+            part, part, ring_send.at[half, core, slot], ring_recv.at[half, core, slot], p, peer * 2 + c
+        )
+
+    def own_copy(core):
+        part = gathered.at[:, z * 2 + core]
+        return remote(part, part, twin_send.at[0], twin_recv.at[0], p, z * 2 + 1 - c)
+
+    def twin_copy(step, core):
+        part = gathered.at[:, pl.ds(origin_of(step, core) * 2, 2)]
+        return remote(part, part, twin_send.at[step], twin_recv.at[step], p, z * 2 + 1 - c)
+
+    for half in range(2):
+        ring_copy(half, c, 0, 0).start()
+    own_copy(c).start()
+    loads[1].wait()
+    loads[2].wait()
 
     @pl.when(p < NBLK)
     def _():
@@ -205,8 +244,12 @@
         known_out[pl.ds(p, 1), pl.ds(z, 1), pl.ds(c, 1)] = inverse[pl.ds(lax.rem(p + 2, K), 1)][:, None, None]
 
     known.start_line()
-
-    home_row, home_half = lax.rem(q, PROWS), q // PROWS
+    own_copy(1 - c).wait_recv()
+    for half in range(2):
+        ring_copy(half, 1 - c, 0, 0).start()
+    loads[3].wait()
+    for j in range(K):
+        adjoint[:, :, j * NB : (j + 1) * NB] = adjoint_raw[:, :, j]
 
     def here_or_there(src, dst, send, recv, row, col, act):
         own = (row == p) & (col == q)
@@ -234,35 +277,27 @@
     def arrived(copy, local):
         copy.wait() if local else copy.wait_recv()
 
-    for half in range(2):
-        move_out(half, start)
 
     def ring_step(step):
-        for half in range(2):
-            ring_wait(0, half, step)
-
-            @pl.when(step < CHIPS // 2)
-            def _():
-                ring_start(0, half, step)
-                ring_wait(1, half, step)
-
-            @pl.when(step < CHIPS // 2 - 1)
-            def _():
-                ring_start(1, half, step)
-
-        twin_copy(lax.rem(z + CHIPS - step, CHIPS), c).start()
-
-        @pl.when(step < CHIPS // 2)
-        def _():
-            twin_copy(lax.rem(z + step, CHIPS), c).start()
+        for core in (c, 1 - c):
+            for half in range(2):
+                ring_copy(half, core, step, step - 1).wait_recv()
+
+                @pl.when(step < steps)
+                def _():
+                    ring_copy(half, core, step, step).start()
+
+        twin_copy(step, c).start()
 
     loop(1, 4, ring_step)
     known.start_flat()
     loop(4, 7, ring_step)
     known.relay()
-    loop(7, CHIPS // 2 + 1, ring_step)
-    loop(0, CHIPS, lambda origin: twin_copy(origin, 1 - c).wait_recv())
-
+    loop(7, steps + 1, ring_step)
+    loop(1, CHIPS // 2 + c, lambda step: twin_copy(step, 1 - c).wait_recv())
+
+    for half in range(2):
+        move_out(half, start)
     everything = gathered[...].reshape(2, NB, K * NB)
     image = inner_product(trail[0], everything[0]) + inner_product(trail[1], everything[1])
     partial[...] = image.reshape(PROWS, 16, K * NB)
@@ -271,7 +306,7 @@
         target = lax.rem(p + step, PROWS)
         return remote(partial.at[target], pieces.at[source], sum_send.at[step], sum_recv.at[source], target, q)
 
-    loop(1, PROWS, lambda step: sum_copy(step, p).start())
+    loop(1, PROWS, lambda index: sum_copy(far_first(index), p).start())
     pieces[pl.ds(p, 1)] = partial[pl.ds(p, 1)]
 
     loop(0, NTOP, known.share)
@@ -314,8 +349,6 @@
             home_row, 2 * p + half, act,
         )
 
-    for half in range(2):
-        home_out(half, start)
     loop(1, 8, lambda step: slice_copy(step, lax.rem(spot + step, 8)).wait_recv())
     tiles[...] = corner[...].reshape(128, 128).T.reshape(16, 8, 128)
 
@@ -328,7 +361,7 @@
             home_row, upper * 16 + k, act,
         )
 
-    loop(0, 16, lambda k: tile_out(k, start))
+    loop(0, 16, lambda k: tile_out(lax.rem(k + p, 16), start))
 
     def tile_in(index):
         j, part = index // 4, lax.rem(index, 4)
@@ -349,14 +382,18 @@
         return remote(terms.at[target], sums.at[source], term_send.at[target], term_recv.at[source], target, q)
 
     def each_term(act):
-        def body(target):
-            @pl.when(target != p)
+        def body(step):
+            target = lax.rem(p + step, PROWS)
+
+            @pl.when(target < NBLK)
             def _():
                 act(term_copy(target, p))
 
-        loop(0, NBLK, body)
+        loop(1, PROWS, body)
 
     each_term(lambda copy: copy.start())
+
+    loads[4].wait()
 
     @pl.when(p < NBLK)
     def _():
@@ -383,6 +420,8 @@
 
     share_column(K - 1)
     share_column(K - 2)
+    for half in range(2):
+        home_out(half, start)
     for j in reversed(range(K)):
         for r in range(j, K):
             opened.finish(block_slot(r, j))
@@ -397,9 +436,10 @@
     low_out[...] = home[...]
 
     for half in range(2):
-        for way in range(2):
-            loop(0, CHIPS // 2 - way, lambda step: ring_copy(way, half, step, step).wait_send())
-    loop(0, CHIPS, lambda origin: twin_copy(origin, c).wait_send())
+        for core in range(2):
+            loop(0, steps, lambda step: ring_copy(half, core, step, step).wait_send())
+    own_copy(c).wait_send()
+    loop(1, steps + 1, lambda step: twin_copy(step, c).wait_send())
     for half in range(2):
         move_out(half, sent)
         home_out(half, sent)
@@ -456,9 +496,16 @@
             jax.ShapeDtypeStruct((2, 8, wide), F32),
             jax.ShapeDtypeStruct((NBLK, 8, NB), F32),
         ],
-        in_specs=[vmem] * 6,
+        in_specs=[vmem] + [pl.BlockSpec(memory_space=pltpu.MemorySpace.HBM)] * 5,
         out_specs=[vmem] * 2,
         scratch_shapes=[
+            pltpu.VMEM((2, 8, K, NB), F32),
+            pltpu.VMEM((2, 8, K, NB), F32),
+            pltpu.VMEM((2, 8, wide), F32),
+            pltpu.VMEM((NBLK, 8, NB), F32),
+            pltpu.VMEM((NBLK, 8, NB), F32),
+            pltpu.VMEM((K, 8, NB), F32),
+            dma((5,)),
             pltpu.VMEM((NTOP, CHIPS, 2, 8, NB), F32),
             pltpu.VMEM((NBLK, CHIPS, 2, 8, NB), F32),
             pltpu.VMEM((NBLK, NB, NB), F32),
@@ -474,18 +521,18 @@
             pltpu.VMEM((PROWS, 8, NB), F32),
             pltpu.VMEM((NBLK, 8, NB), F32),
             pltpu.VMEM((2, 8, wide), F32),
-            dma((2, 2, 8)), dma((2, 2, 8)), dma((CHIPS,)), dma((CHIPS,)), dma((2,)), dma((2,)),
+            dma((2, 2, 8)), dma((2, 2, 8)), dma((9,)), dma((9,)), dma((2,)), dma((2,)),
             dma((PROWS,)), dma((PROWS,)), dma((2,)), dma((2,)), dma((8,)), dma((8,)),
             dma((16,)), dma((4, 4)), dma((NBLK,)), dma((PROWS,)),
             *spread_sems(NTOP),
             *spread_sems(NBLK),
         ],
-        compiler_params=pltpu.CompilerParams(has_side_effects=True, vmem_limit_bytes=40 * 1024 * 1024),
+        compiler_params=pltpu.CompilerParams(collective_id=0, has_side_effects=True, vmem_limit_bytes=40 * 1024 * 1024),
         name="exchange",
     )(
         adjoint_trail.reshape(2, NB, NB),
-        factor_low.reshape(2, 8, wide),
-        adjoint_low.reshape(2, 8, wide),
+        factor_low.reshape(2, 8, K, NB),
+        adjoint_low.reshape(2, 8, K, NB),
         factor_top,
         adjoint_top,
         diag_inverse,

time: 162 us -> 143 us (0.88)
  Pallas kernels: 157 us -> 139 us
    pallas_call x1, Pallas kernels: 157 us -> 139 us  [per_device(): pl.pallas_call(exchange_kernel, out_shape=[jax.ShapeDtypeStruct((2, 8, wi...]
where the time goes in v3:
time: 143 us; the launch traced here: 142 us
  Pallas kernels  139 us (97%)
  local copies, waits for them, and re-layouts  2.46 us (2%)
    pallas_call x1, Pallas kernels, per_device(): pl.pallas_call(exchange_kernel, out_shape=[jax.ShapeDtypeStruct((2, 8, wi...  139 us

profile of v3, /device:TPU:7, one launch (start us, length us, event | category | flops | bytes accessed | tf_op | source)
XLA Modules:
  0.0 142.0 jit_solution(16204131554991425933)
XLA Ops:
  0.6 0.0 copy-start
  0.6 0.0 copy-start.1
  0.7 0.0 copy-start.2
  0.7 0.0 copy-start.3
  0.7 0.0 copy-start.4
  0.7 1.1 copy.11
  1.8 0.0 copy-done
  1.8 0.0 copy-done.1
  1.8 0.0 copy-done.2
  1.9 0.0 copy-done.3
  1.9 0.0 copy-done.4
  1.9 138.8 %exchange.1 = (f32[2,8,1024]{2,1,0:T(8,128)S(1)}, f32[10,8,256]{2,1,0:T(8,128)S(1)}) custom-call(f32[2,256,256]{2,1,0:T(8,128)S(1)} %bitcast.6, f32[2,8,4,256]{3,2,1,0:T(4,128)S(1)} %bitcast.8, f32[2,8,4,256]{3,2,1,0:T(4,128)S(1)} %bitcast.9, f32[10,8,256]{2,1,0:T(8,128)S(1)} %copy-done, f32[10,8,256]{2,1,0:T(8,128)S(1)} %copy-done.1, f32[4,8,256]{2,1,0:T(8,128)S(1)} %copy-done.4), custom_call_target="tpu_custom_call" | custom-call | tf_op jit(solution)/shard_map/exchange/pallas_call | solution.py:493
  140.7 0.7 copy.8
  141.4 0.6 copy.13
Async XLA Ops:
  0.6 1.2 copy-start
  0.6 1.2 copy-start.1
  0.7 1.2 copy-start.2
  0.7 1.2 copy-start.3
  0.7 1.2 copy-start.4

commit v4 on v3

--- a/solution.py
+++ b/solution.py
@@ -14,19 +14,31 @@
 CHIPS = 16
 SIDE = 4
 
-HIGHEST = lax.Precision.HIGHEST
 MESH = pl.DeviceIdType.MESH
 F32 = jnp.float32
+BF16 = jnp.bfloat16
+
+
+def split(array):
+    high = array.astype(BF16)
+    return high, (array - high.astype(F32)).astype(BF16)
+
+
+def product(left, right, dims):
+    (a, a_rest), (b, b_rest) = split(left), split(right)
+
+    def dot(x, y):
+        return lax.dot_general(x, y, (dims, ((), ())), preferred_element_type=F32)
+
+    return dot(a, b) + (dot(a, b_rest) + dot(a_rest, b))
 
 
 def matmul(left, right):
-    return jnp.dot(left, right, precision=HIGHEST, preferred_element_type=F32)
+    return product(left, right, ((1,), (0,)))
 
 
 def inner_product(left, right):
-    return lax.dot_general(
-        left, right, (((0,), (0,)), ((), ())), precision=HIGHEST, preferred_element_type=F32
-    )
+    return product(left, right, ((0,), (0,)))
 
 
 def block_slot(row_block, col_block):

time: 143 us -> 138 us (0.965)
  the two profiles are of different devices: /device:TPU:7 before, /device:TPU:17 now
where the time goes in v4:
time: 138 us
  Pallas kernels  134 us (97%)
  local copies, waits for them, and re-layouts  2.46 us (2%)
    pallas_call x1, Pallas kernels, per_device(): pl.pallas_call(exchange_kernel, out_shape=[jax.ShapeDtypeStruct((2, 8, wi...  134 us

profile of v4, /device:TPU:17, one launch (start us, length us, event | category | flops | bytes accessed | tf_op | source)
XLA Modules:
  0.0 137.5 jit_solution(6864821161311784282)
XLA Ops:
  0.6 0.0 copy-start
  0.6 0.0 copy-start.1
  0.7 0.0 copy-start.2
  0.7 0.0 copy-start.3
  0.7 0.0 copy-start.4
  0.7 1.1 copy.11
  1.8 0.0 copy-done
  1.8 0.0 copy-done.1
  1.8 0.0 copy-done.2
  1.9 0.0 copy-done.3
  1.9 0.0 copy-done.4
  1.9 134.4 %exchange.1 = (f32[2,8,1024]{2,1,0:T(8,128)S(1)}, f32[10,8,256]{2,1,0:T(8,128)S(1)}) custom-call(f32[2,256,256]{2,1,0:T(8,128)S(1)} %bitcast.6, f32[2,8,4,256]{3,2,1,0:T(4,128)S(1)} %bitcast.8, f32[2,8,4,256]{3,2,1,0:T(4,128)S(1)} %bitcast.9, f32[10,8,256]{2,1,0:T(8,128)S(1)} %copy-done, f32[10,8,256]{2,1,0:T(8,128)S(1)} %copy-done.1, f32[4,8,256]{2,1,0:T(8,128)S(1)} %copy-done.4), custom_call_target="tpu_custom_call" | custom-call | tf_op jit(solution)/shard_map/exchange/pallas_call | solution.py:505
  136.2 0.7 copy.8
  136.9 0.6 copy.13
Async XLA Ops:
  0.6 1.2 copy-start
  0.6 1.2 copy-start.1
  0.7 1.2 copy-start.2
  0.7 1.2 copy-start.3
  0.7 1.2 copy-start.4

commit v5 on v4

--- a/solution.py
+++ b/solution.py
@@ -110,11 +110,10 @@
         def _():
             loop(1, CHIPS, lambda step: self.line_copy(step, lax.rem(z + step, CHIPS)).wait_recv())
 
-            def body(step):
+            for step in (1, 3, 2):
                 self.near_copy(step).start()
+            for step in (1, 3, 2):
                 self.far_copy(p, 0, step).start()
-
-            loop(1, SIDE, body)
             self.twin_copy(p, c).start()
 
     def relay(self):
@@ -124,9 +123,11 @@
             @pl.when(block < self.count)
             def _():
                 self.far_copy(block, origin, 1).wait_recv()
-                loop(1, SIDE, lambda step: self.far_copy(block, origin, step).start())
-
-        loop(1, SIDE, body)
+                for step in (1, 3, 2):
+                    self.far_copy(block, origin, step).start()
+
+        for origin in (1, 3, 2):
+            body(origin)
 
     def share(self, block):
         p, z, c = self.place
@@ -318,7 +319,7 @@
         target = lax.rem(p + step, PROWS)
         return remote(partial.at[target], pieces.at[source], sum_send.at[step], sum_recv.at[source], target, q)
 
-    loop(1, PROWS, lambda index: sum_copy(far_first(index), p).start())
+    loop(1, PROWS, lambda index: sum_copy(index, p).start())
     pieces[pl.ds(p, 1)] = partial[pl.ds(p, 1)]
 
     loop(0, NTOP, known.share)
@@ -430,16 +431,14 @@
         for r in range(j, K):
             opened.share(block_slot(r, j))
 
-    share_column(K - 1)
-    share_column(K - 2)
+    for j in reversed(range(K)):
+        share_column(j)
     for half in range(2):
         home_out(half, start)
     for j in reversed(range(K)):
         for r in range(j, K):
             opened.finish(block_slot(r, j))
         top_column(j, known_out, open_out, full)
-        if j >= 2:
-            share_column(j - 2)
     top_out[...] = full[:, pl.ds(pl.multiple_of(q * 8, 8), 8), :]
     for half in range(2):
         here_or_there(

time: 138 us -> 134 us (0.971)
  the two profiles are of different devices: /device:TPU:17 before, /device:TPU:7 now
where the time goes in v5:
time: 134 us
  Pallas kernels  131 us (98%)
  local copies, waits for them, and re-layouts  2.46 us (2%)
    pallas_call x1, Pallas kernels, per_device(): pl.pallas_call(exchange_kernel, out_shape=[jax.ShapeDtypeStruct((2, 8, wi...  131 us

profile of v5, /device:TPU:7, one launch (start us, length us, event | category | flops | bytes accessed | tf_op | source)
XLA Modules:
  0.0 134.1 jit_solution(8324193666298697691)
XLA Ops:
  0.6 0.0 copy-start
  0.6 0.0 copy-start.1
  0.7 0.0 copy-start.2
  0.7 0.0 copy-start.3
  0.7 0.0 copy-start.4
  0.7 1.1 copy.11
  1.8 0.0 copy-done
  1.8 0.0 copy-done.1
  1.8 0.0 copy-done.2
  1.9 0.0 copy-done.3
  1.9 0.0 copy-done.4
  1.9 130.9 %exchange.1 = (f32[2,8,1024]{2,1,0:T(8,128)S(1)}, f32[10,8,256]{2,1,0:T(8,128)S(1)}) custom-call(f32[2,256,256]{2,1,0:T(8,128)S(1)} %bitcast.6, f32[2,8,4,256]{3,2,1,0:T(4,128)S(1)} %bitcast.8, f32[2,8,4,256]{3,2,1,0:T(4,128)S(1)} %bitcast.9, f32[10,8,256]{2,1,0:T(8,128)S(1)} %copy-done, f32[10,8,256]{2,1,0:T(8,128)S(1)} %copy-done.1, f32[4,8,256]{2,1,0:T(8,128)S(1)} %copy-done.4), custom_call_target="tpu_custom_call" | custom-call | tf_op jit(solution)/shard_map/exchange/pallas_call | solution.py:504
  132.8 0.7 copy.8
  133.4 0.6 copy.13
Async XLA Ops:
  0.6 1.2 copy-start
  0.6 1.2 copy-start.1
  0.7 1.2 copy-start.2
  0.7 1.2 copy-start.3
  0.7 1.2 copy-start.4

commit v6 on v5

--- a/solution.py
+++ b/solution.py
@@ -26,11 +26,9 @@
 
 def product(left, right, dims):
     (a, a_rest), (b, b_rest) = split(left), split(right)
-
-    def dot(x, y):
-        return lax.dot_general(x, y, (dims, ((), ())), preferred_element_type=F32)
-
-    return dot(a, b) + (dot(a, b_rest) + dot(a_rest, b))
+    longer = jnp.concatenate([a, a, a_rest], axis=dims[0][0])
+    taller = jnp.concatenate([b, b_rest, b], axis=dims[1][0])
+    return lax.dot_general(longer, taller, (dims, ((), ())), preferred_element_type=F32)
 
 
 def matmul(left, right):

time: 134 us -> 134 us (level)
  no operation moved by 1% of the time
where the time goes in v6:
time: 134 us
  Pallas kernels  131 us (98%)
  local copies, waits for them, and re-layouts  2.46 us (2%)
    pallas_call x1, Pallas kernels, per_device(): pl.pallas_call(exchange_kernel, out_shape=[jax.ShapeDtypeStruct((2, 8, wi...  131 us

profile of v6, /device:TPU:7, one launch (start us, length us, event | category | flops | bytes accessed | tf_op | source)
XLA Modules:
  0.0 133.8 jit_solution(8771001942478743322)
XLA Ops:
  0.6 0.0 copy-start
  0.6 0.0 copy-start.1
  0.7 0.0 copy-start.2
  0.7 0.0 copy-start.3
  0.7 0.0 copy-start.4
  0.7 1.1 copy.11
  1.8 0.0 copy-done
  1.8 0.0 copy-done.1
  1.8 0.0 copy-done.2
  1.9 0.0 copy-done.3
  1.9 0.0 copy-done.4
  1.9 130.6 %exchange.1 = (f32[2,8,1024]{2,1,0:T(8,128)S(1)}, f32[10,8,256]{2,1,0:T(8,128)S(1)}) custom-call(f32[2,256,256]{2,1,0:T(8,128)S(1)} %bitcast.6, f32[2,8,4,256]{3,2,1,0:T(4,128)S(1)} %bitcast.8, f32[2,8,4,256]{3,2,1,0:T(4,128)S(1)} %bitcast.9, f32[10,8,256]{2,1,0:T(8,128)S(1)} %copy-done, f32[10,8,256]{2,1,0:T(8,128)S(1)} %copy-done.1, f32[4,8,256]{2,1,0:T(8,128)S(1)} %copy-done.4), custom_call_target="tpu_custom_call" | custom-call | tf_op jit(solution)/shard_map/exchange/pallas_call | solution.py:502
  132.5 0.7 copy.8
  133.1 0.6 copy.13
Async XLA Ops:
  0.6 1.2 copy-start
  0.6 1.2 copy-start.1
  0.7 1.2 copy-start.2
  0.7 1.2 copy-start.3
  0.7 1.2 copy-start.4
